TPU v7x, 128 devices: a whole 4x4x4 slice. The times are simulated.
128 devices in a mesh: row: 16 (over y, z), col: 8 (over x, core).
Axes of the slice: x: 4, y: 4, z: 4, core: 2. Of those that a mesh axis runs over, the one named last changes fastest.
Arguments:
- tokens: bfloat16 [2048, 4096], P('row', 'col'), may hold values from -6 to 6
- w_in: bfloat16 [4096, 16384], P('col', 'row'), may hold values from -0.09375 to 0.09375
- w_out: bfloat16 [16384, 4096], P('row', 'col'), may hold values from -0.046875 to 0.046875
- cotangent: bfloat16 [2048, 4096], P('row', 'col'), may hold values from -6 to 6
Outputs:
- block_out: bfloat16 [2048, 4096], P(('row', 'col'))
- grad_tokens: bfloat16 [2048, 4096], P('row', 'col')
- grad_in: float32 [4096, 16384], P('col', 'row')
- grad_out: float32 [16384, 4096], P('row', 'col')
All inputs are finite; a program needn't handle non-finite values.
Results may differ from a plain program's by a relative error of at most 0.015.
Values may be sent and summed in bfloat16 or wider, within the bound.
A program may use at most 128 MiB of HBM per device.

v0:
```python
import jax
import jax.numpy as jnp
from jax import lax
from jax.sharding import PartitionSpec as P


def gelu_grad(value):
    cdf = 0.5 * (1.0 + jax.scipy.special.erf(value * 0.7071067811865476))
    pdf = jnp.exp(-0.5 * value * value) * 0.3989422804014327
    return cdf + value * pdf


def token_panel(local_rows):
    return lax.all_gather(local_rows, "row", axis=0, tiled=True)


def token_panel_a2a(local_rows):
    n = lax.axis_size("row")
    copies = jnp.broadcast_to(local_rows[None], (n,) + local_rows.shape)
    copies = copies.reshape(n * local_rows.shape[0], local_rows.shape[1])
    return lax.all_to_all(copies, "row", split_axis=0, concat_axis=0, tiled=True)


def hidden_panel(local_rows):
    return lax.all_gather(local_rows, "col", axis=0, tiled=True)


def contract_last(left, right):
    return lax.dot_general(
        left, right, (((1,), (1,)), ((), ())), preferred_element_type=jnp.float32
    )


def width_split(left_all, right, transposed):
    if transposed:
        term = contract_last(left_all, right)
    else:
        term = jnp.dot(left_all, right, preferred_element_type=jnp.float32)
    return lax.psum_scatter(
        term.astype(jnp.bfloat16), "col", scatter_dimension=0, tiled=True
    ).astype(jnp.float32)


def unit_sum(left_all, right, transposed):
    n = lax.axis_size("row")
    if transposed:
        term = contract_last(left_all, right)
    else:
        term = jnp.dot(left_all, right, preferred_element_type=jnp.float32)
    pieces = term.astype(jnp.bfloat16).reshape(n, term.shape[0] // n, term.shape[1])
    pieces = lax.all_to_all(pieces, "row", split_axis=0, concat_axis=0, tiled=True)
    return jnp.sum(pieces.astype(jnp.float32), axis=0)


def local(tokens, w_in, w_out, cotangent):
    tokens_all = token_panel(tokens)
    upstream_all = token_panel_a2a(cotangent)
    pre_part = width_split(tokens_all, w_in, False)
    act_all = hidden_panel(jax.nn.gelu(pre_part, approximate=False).astype(jnp.bfloat16))
    dact_part = width_split(upstream_all, w_out, True)
    dpre_all = hidden_panel((dact_part * gelu_grad(pre_part)).astype(jnp.bfloat16))
    mixed = unit_sum(act_all, w_out, False)
    block_rows = (tokens.astype(jnp.float32) + mixed).astype(jnp.bfloat16)
    block_out = lax.all_to_all(block_rows, "col", split_axis=0, concat_axis=1, tiled=True)
    grad_out = lax.dot_general(
        act_all, upstream_all, (((0,), (0,)), ((), ())), preferred_element_type=jnp.float32
    )
    grad_in = lax.dot_general(
        tokens_all, dpre_all, (((0,), (0,)), ((), ())), preferred_element_type=jnp.float32
    )
    back = unit_sum(dpre_all, w_in, True)
    grad_tokens = (cotangent.astype(jnp.float32) + back).astype(jnp.bfloat16)
    return (block_out, grad_tokens, grad_in, grad_out)


def solution(mesh):
    in_specs = (P("row", "col"), P("col", "row"), P("row", "col"), P("row", "col"))
    out_specs = (P(("row", "col"), None), P("row", "col"), P("col", "row"), P("row", "col"))
    return jax.shard_map(local, mesh=mesh, in_specs=in_specs, out_specs=out_specs, check_vma=False)
```

profile of v0, /device:TPU:1, one launch (start us, length us, event | category | flops | bytes accessed | tf_op | source)
XLA Modules:
  0.0 260.2 jit_solution(16874489885100301524)
XLA Ops:
  8.0 0.0 copy-start
  8.0 0.0 all-gather.4.cloned.1.call-start
  8.1 0.7 all-gather.4.cloned.1.call-update
  8.7 0.0 reduce-scatter.5.cloned.1.call-start
  8.8 1.1 broadcast_in_dim.2
  9.9 37.6 %all_to_all.38 = bf16[16,128,512]{2,1,0:T(8,128)(2,1)S(1)} all-to-all(bf16[16,128,512]{2,1,0:T(8,128)(2,1)S(1)} %broadcast_in_dim.2), channel_id=1, replica_groups=mesh['row'=16,'col'=8] {'row'}, dimensions={0} | all-to-all | bytes 4194304 | tf_op jit(solution)/shard_map/all_to_all | solution.py:21
  47.5 0.0 copy-start.1
  47.5 1.4 copy-done.1
  48.9 0.0 copy-done
  48.9 4.3 %convolution_convert_fusion = bf16[2048,1024]{1,0:T(8,128)(2,1)} fusion(bf16[2048,512]{1,0:T(8,128)(2,1)S(1)} %bitcast.21, bf16[1024,512]{1,0:T(8,128)(2,1)S(1)} %copy-done), kind=kOutput, calls=%fused_computation.2 | convolution fusion | flops 2149580800 | bytes 7340032 | tf_op jit(solution)/shard_map/dot_general | solution.py:29
  53.2 0.0 copy-start.4
  53.2 0.0 reduce-scatter.5.cloned.1.call-update
  53.3 0.0 reduce-scatter.3.cloned.1.call-start
  53.3 12.5 %all-gather.4.cloned.1.call-done = bf16[2048,512]{1,0:T(8,128)(2,1)} async-done(((bf16[128,512]{1,0:T(8,128)(2,1)}), bf16[2048,512]{1,0:T(8,128)(2,1)}) %all-gather.4.cloned.1.call-update) | async-done | bytes 2097168 | tf_op jit(solution)/shard_map/all_gather | solution.py:14
  65.8 0.0 copy-done.4
  65.8 5.9 %convolution_convert_fusion.1 = bf16[2048,1024]{1,0:T(8,128)(2,1)} fusion(bf16[2048,512]{1,0:T(8,128)(2,1)} %all-gather.4.cloned.1.call-done, bf16[512,1024]{1,0:T(8,128)(2,1)S(1)} %copy-done.4), kind=kOutput, calls=%fused_computation.3 | convolution fusion | flops 2149580800 | bytes 7340032 | tf_op jit(solution)/shard_map/dot_general | solution.py:38
  71.8 0.0 reduce-scatter.3.cloned.1.call-update
  71.8 0.0 all-gather.6.cloned.1.call-start
  71.9 15.8 %reduce-scatter.5.cloned.1.call-done = bf16[256,1024]{1,0:T(8,128)(2,1)} async-done(((bf16[2048,1024]{1,0:T(8,128)(2,1)}), bf16[256,1024]{1,0:T(8,128)(2,1)}) %reduce-scatter.5.cloned.1.call-update) | async-done | bytes 524304 | tf_op jit(solution)/shard_map/reduce_scatter | solution.py:39
  87.7 38.8 %reduce-scatter.3.cloned.1.call-done = bf16[256,1024]{1,0:T(8,128)(2,1)} async-done(((bf16[2048,1024]{1,0:T(8,128)(2,1)}), bf16[256,1024]{1,0:T(8,128)(2,1)}) %reduce-scatter.3.cloned.1.call-update) | async-done | bytes 524304 | tf_op jit(solution)/shard_map/reduce_scatter | solution.py:39
  126.4 4.6 %fusion.38 = (bf16[256,1024]{1,0:T(8,128)(2,1)}, bf16[256,1024]{1,0:T(8,128)(2,1)}) fusion(bf16[256,1024]{1,0:T(8,128)(2,1)} %reduce-scatter.3.cloned.1.call-done, bf16[256,1024]{1,0:T(8,128)(2,1)} %reduce-scatter.5.cloned.1.call-done), kind=kLoop, calls=%fused_computation.52 | loop fusion | flops 20185088 | bytes 2097152 | tf_op jit(solution)/shard_map/convert_element_type | solution.py:61
  131.0 0.0 all-gather.6.cloned.1.call-update
  131.0 0.0 all-gather.8.cloned.1.call-start
  131.1 0.7 all-gather.8.cloned.1.call-update
  131.8 33.5 %all-gather.6.cloned.1.call-done = bf16[2048,1024]{1,0:T(8,128)(2,1)} async-done(((bf16[256,1024]{1,0:T(8,128)(2,1)}), bf16[2048,1024]{1,0:T(8,128)(2,1)}) %all-gather.6.cloned.1.call-update) | async-done | bytes 4194320 | tf_op jit(solution)/shard_map/all_gather | solution.py:25
  165.3 5.8 %convolution_convert_fusion.3 = bf16[2048,512]{1,0:T(8,128)(2,1)} fusion(bf16[2048,1024]{1,0:T(8,128)(2,1)} %all-gather.6.cloned.1.call-done, bf16[1024,512]{1,0:T(8,128)(2,1)S(1)} %copy-done), kind=kOutput, calls=%fused_computation.5 | convolution fusion | flops 2148532224 | bytes 7340032 | tf_op jit(solution)/shard_map/dot_general | solution.py:49
  171.1 6.7 %all-to-all-start = ((bf16[16,128,512]{2,1,0:T(8,128)(2,1)}), bf16[16,128,512]{2,1,0:T(8,128)(2,1)S(1)}, u32[]{:S(2)}, u32[]{:S(2)}) async-start(bf16[16,128,512]{2,1,0:T(8,128)(2,1)} %bitcast.24), calls=%async_computation.1 | async-start | bytes 4194304 | tf_op jit(solution)/shard_map/all_to_all | solution.py:51
  177.9 21.7 %all-gather.8.cloned.1.call-done = bf16[2048,1024]{1,0:T(8,128)(2,1)} async-done(((bf16[256,1024]{1,0:T(8,128)(2,1)}), bf16[2048,1024]{1,0:T(8,128)(2,1)}) %all-gather.8.cloned.1.call-update) | async-done | bytes 4194320 | tf_op jit(solution)/shard_map/all_gather | solution.py:25
  199.5 6.2 %convolution_convert_fusion.2 = bf16[2048,512]{1,0:T(8,128)(2,1)} fusion(bf16[2048,1024]{1,0:T(8,128)(2,1)} %all-gather.8.cloned.1.call-done, bf16[512,1024]{1,0:T(8,128)(2,1)} %param.5), kind=kOutput, calls=%fused_computation.4 | convolution fusion | flops 2148532224 | bytes 7340032 | tf_op jit(solution)/shard_map/dot_general | solution.py:29
  205.7 1.4 all-to-all-done
  207.1 5.4 %all-to-all-start.3 = ((bf16[16,128,512]{2,1,0:T(8,128)(2,1)}), bf16[16,128,512]{2,1,0:T(8,128)(2,1)}, u32[]{:S(2)}, u32[]{:S(2)}) async-start(bf16[16,128,512]{2,1,0:T(8,128)(2,1)} %bitcast.23), calls=%async_computation.5 | async-start | bytes 4194304 | tf_op jit(solution)/shard_map/all_to_all | solution.py:51
  212.5 6.6 %convolution_bitcast_fusion = f32[512,1024]{0,1:T(8,128)} fusion(bf16[2048,1024]{1,0:T(8,128)(2,1)} %all-gather.8.cloned.1.call-done, bf16[2048,512]{1,0:T(8,128)(2,1)} %all-gather.4.cloned.1.call-done), kind=kOutput, calls=%fused_computation.12 | convolution fusion | flops 2147483648 | bytes 8388608 | tf_op jit(solution)/shard_map/dot_general | solution.py:68
  219.0 2.9 %copy.12 = f32[512,1024]{1,0:T(8,128)} copy(f32[512,1024]{0,1:T(8,128)} %convolution_bitcast_fusion) | data formatting | bytes 4194304
  221.9 6.5 %fusion.39 = f32[1024,512]{1,0:T(8,128)} fusion(bf16[2048,1024]{1,0:T(8,128)(2,1)} %all-gather.6.cloned.1.call-done, bf16[2048,512]{1,0:T(8,128)(2,1)} %bitcast.22), kind=kOutput, calls=%fused_computation.55 | convolution fusion | flops 2147483648 | bytes 8388608 | tf_op jit(solution)/shard_map/dot_general | solution.py:65
  228.5 0.0 copy-start.3
  228.5 0.3 convert_reduce_fusion.1
  228.8 0.6 copy-done.3
  229.4 0.0 copy-start.2
  229.4 0.7 add_convert_fusion.1
  230.0 8.0 %all-to-all-done.3 = bf16[16,128,512]{2,1,0:T(8,128)(2,1)} async-done(((bf16[16,128,512]{2,1,0:T(8,128)(2,1)}), bf16[16,128,512]{2,1,0:T(8,128)(2,1)}, u32[]{:S(2)}, u32[]{:S(2)}) %all-to-all-start.3) | async-done | bytes 2097184 | tf_op jit(solution)/shard_map/all_to_all | solution.py:51
  238.1 8.6 %all-to-all-start.1 = ((bf16[8,16,512]{2,1,0:T(8,128)(2,1)}), bf16[8,16,512]{2,1,0:T(8,128)(2,1)S(1)}, u32[]{:S(2)}, u32[]{:S(2)}) async-start(bf16[8,16,512]{2,1,0:T(8,128)(2,1)} %bitcast.1), calls=%async_computation.2 | async-start | bytes 262144 | tf_op jit(solution)/shard_map/all_to_all | solution.py:64
  246.7 1.9 convert_reduce_fusion
  248.6 0.0 copy-done.2
  248.6 0.7 add_convert_fusion
  249.3 2.7 %all-to-all-done.1 = bf16[8,16,512]{2,1,0:T(8,128)(2,1)S(1)} async-done(((bf16[8,16,512]{2,1,0:T(8,128)(2,1)}), bf16[8,16,512]{2,1,0:T(8,128)(2,1)S(1)}, u32[]{:S(2)}, u32[]{:S(2)}) %all-to-all-start.1) | async-done | bytes 131104 | tf_op jit(solution)/shard_map/all_to_all | solution.py:64
  252.0 0.7 copy.13
Async XLA Ops:
  8.0 40.9 %copy-start = (bf16[1024,512]{1,0:T(8,128)(2,1)S(1)}, bf16[1024,512]{1,0:T(8,128)(2,1)}, u32[]{:S(2)}) copy-start(bf16[1024,512]{1,0:T(8,128)(2,1)} %param.6) | copy-start | bytes 3145732
  8.0 57.8 %all-gather.4.cloned.1.call-start = ((), (), s32[]{:S(2)}) async-start(), calls=%async_computation.6 | async-start | bytes 2228224 | tf_op jit(solution)/shard_map/all_gather | solution.py:14
  8.7 78.9 %reduce-scatter.5.cloned.1.call-start = ((), (), s32[]{:S(2)}) async-start(), calls=%async_computation.9 | async-start | bytes 4718592 | tf_op jit(solution)/shard_map/reduce_scatter | solution.py:39
  47.5 1.4 copy-start.1
  53.2 12.6 %copy-start.4 = (bf16[512,1024]{1,0:T(8,128)(2,1)S(1)}, bf16[512,1024]{1,0:T(8,128)(2,1)}, u32[]{:S(2)}) copy-start(bf16[512,1024]{1,0:T(8,128)(2,1)} %param.5) | copy-start | bytes 3145732
  53.3 73.2 %reduce-scatter.3.cloned.1.call-start = ((), (), s32[]{:S(2)}) async-start(), calls=%async_computation.7 | async-start | bytes 4718592 | tf_op jit(solution)/shard_map/reduce_scatter | solution.py:39
  71.8 93.5 %all-gather.6.cloned.1.call-start = ((), (), s32[]{:S(2)}) async-start(), calls=%async_computation.8 | async-start | bytes 4718592 | tf_op jit(solution)/shard_map/all_gather | solution.py:25
  131.0 68.5 %all-gather.8.cloned.1.call-start = ((), (), s32[]{:S(2)}) async-start(), calls=%async_computation.10 | async-start | bytes 4718592 | tf_op jit(solution)/shard_map/all_gather | solution.py:25
  171.1 35.9 %all-to-all-start = ((bf16[16,128,512]{2,1,0:T(8,128)(2,1)}), bf16[16,128,512]{2,1,0:T(8,128)(2,1)S(1)}, u32[]{:S(2)}, u32[]{:S(2)}) async-start(bf16[16,128,512]{2,1,0:T(8,128)(2,1)} %bitcast.24), calls=%async_computation.1 | async-start | bytes 4194304 | tf_op jit(solution)/shard_map/all_to_all | solution.py:51
  207.1 31.0 %all-to-all-start.3 = ((bf16[16,128,512]{2,1,0:T(8,128)(2,1)}), bf16[16,128,512]{2,1,0:T(8,128)(2,1)}, u32[]{:S(2)}, u32[]{:S(2)}) async-start(bf16[16,128,512]{2,1,0:T(8,128)(2,1)} %bitcast.23), calls=%async_computation.5 | async-start | bytes 4194304 | tf_op jit(solution)/shard_map/all_to_all | solution.py:51
  228.5 0.9 copy-start.3
  229.4 19.2 %copy-start.2 = (bf16[128,512]{1,0:T(8,128)(2,1)S(1)}, bf16[128,512]{1,0:T(8,128)(2,1)}, u32[]{:S(2)}) copy-start(bf16[128,512]{1,0:T(8,128)(2,1)} %param.7) | copy-start | bytes 393220
  238.1 13.9 %all-to-all-start.1 = ((bf16[8,16,512]{2,1,0:T(8,128)(2,1)}), bf16[8,16,512]{2,1,0:T(8,128)(2,1)S(1)}, u32[]{:S(2)}, u32[]{:S(2)}) async-start(bf16[8,16,512]{2,1,0:T(8,128)(2,1)} %bitcast.1), calls=%async_computation.2 | async-start | bytes 262144 | tf_op jit(solution)/shard_map/all_to_all | solution.py:64
Sparse Core Ops, SparseCore 0:
  11.0 54.8 all-gather.3
Sparse Core Ops, SparseCore 1:
  53.4 34.3 reduce-scatter.4
  89.9 36.4 reduce-scatter.2
  131.1 34.1 all-gather.5
  167.6 31.9 all-gather.7
where the time goes:
time: 261 us; the launch traced here: 260 us
  waiting for transfers between devices  136 us (52%)
  blocking collectives  37.6 us (14%)
  matrix products  35.4 us (14%)
  starting transfers between devices  20.9 us (8%)
  between operations  15.7 us (6%)
  other arithmetic  8.13 us (3%)
  local copies, waits for them, and re-layouts  6.64 us (3%)
    all_gather x2, waiting for transfers between devices, hidden_panel(): return lax.all_gather(local_rows, 'col', axis=0, tiled=True)  55.2 us
    reduce_scatter x2, waiting for transfers between devices, width_split(): lax.psum_scatter(term.astype(jnp.bfloat16), 'col', scatter_dimension=0, t...  54.6 us
    all_to_all x1, blocking collectives, token_panel_a2a(): lax.all_to_all(copies, 'row', split_axis=0, concat_axis=0, tiled=True)  37.6 us
    all_gather x1, waiting for transfers between devices, token_panel(): return lax.all_gather(local_rows, 'row', axis=0, tiled=True)  12.5 us
    all_to_all x2, starting transfers between devices, unit_sum(): lax.all_to_all(pieces, 'row', split_axis=0, concat_axis=0, tiled=True)  12.1 us
    dot_general x2, matrix products, contract_last(): lax.dot_general(left, right, (((1,), (1,)), ((), ())), preferred_element_...  10.5 us
    all_to_all x2, waiting for transfers between devices, unit_sum(): lax.all_to_all(pieces, 'row', split_axis=0, concat_axis=0, tiled=True)  9.4 us
    all_to_all x1, starting transfers between devices, local(): lax.all_to_all(block_rows, 'col', split_axis=0, concat_axis=1, tiled=True)  8.57 us
  transfers between devices with their start and end apart: 8, of which 8 were waited for; matrix products, arithmetic and copies ran while one was open for 17% of the time, Pallas kernels for 0%

commit v1 on v0

--- a/solution.py
+++ b/solution.py
@@ -2,6 +2,22 @@
 import jax.numpy as jnp
 from jax import lax
 from jax.sharding import PartitionSpec as P
+
+
+def collect(x, axis, dim):
+    ways, here, step = (lax.axis_size(axis), lax.axis_index(axis), x.shape[dim])
+    dims = [n * ways if d == dim else n for d, n in enumerate(x.shape)]
+    full = lax.dynamic_update_slice_in_dim(jnp.zeros(dims, x.dtype), x, here * step, axis=dim)
+    going_up = going_down = x
+    for far in range(1, ways // 2 + 1):
+        going_up = lax.ppermute(going_up, axis, [(d, (d + 1) % ways) for d in range(ways)])
+        full = lax.dynamic_update_slice_in_dim(full, going_up, (here - far) % ways * step, axis=dim)
+        if 2 * far < ways:
+            going_down = lax.ppermute(going_down, axis, [(d, (d - 1) % ways) for d in range(ways)])
+            full = lax.dynamic_update_slice_in_dim(
+                full, going_down, (here + far) % ways * step, axis=dim
+            )
+    return full
 
 
 def gelu_grad(value):
@@ -22,7 +38,7 @@
 
 
 def hidden_panel(local_rows):
-    return lax.all_gather(local_rows, "col", axis=0, tiled=True)
+    return collect(local_rows, "col", 0)
 
 
 def contract_last(left, right):

time: 261 us -> 272 us (1.042)
  waiting for transfers between devices: 136 us -> 97.4 us
  starting transfers between devices: 20.9 us -> 56.7 us
  local copies, waits for them, and re-layouts: 6.64 us -> 28.9 us
  blocking collectives: 37.6 us -> 30.7 us
    all_gather x2 -> x0, waiting for transfers between devices: 55.2 us -> none  [hidden_panel(): return lax.all_gather(local_rows, 'col', axis=0, tiled=True)]
    all_gather x1, waiting for transfers between devices: 12.5 us -> 49.7 us  [token_panel(): return lax.all_gather(local_rows, 'row', axis=0, tiled=True)]
    reduce_scatter x2, waiting for transfers between devices: 54.6 us -> 22.3 us  [width_split(): lax.psum_scatter(term.astype(jnp.bfloat16), 'col', scatter_dimension=0, t...]
    ppermute x0 -> x14, starting transfers between devices: none -> 26.6 us  [the longest x8 14.7 us: collect(): lax.ppermute(going_up, axis, [(d, (d + 1) % ways) for d in range(ways)])]
    ppermute x0 -> x14, waiting for transfers between devices: none -> 20.3 us  [the longest x8 13.2 us: collect(): lax.ppermute(going_up, axis, [(d, (d + 1) % ways) for d in range(ways)])]
    dynamic_update_slice x0 -> x14, local copies, waits for them, and re-layouts: none -> 18 us  [the longest x8 10.9 us: collect(): lax.dynamic_update_slice_in_dim(full, going_up, (here - far) % ways * ste...]
    all_to_all x1, starting transfers between devices: 8.57 us -> 18.8 us  [local(): lax.all_to_all(block_rows, 'col', split_axis=0, concat_axis=1, tiled=True)]
    all_to_all x2, waiting for transfers between devices: 9.4 us -> 1.73 us  [unit_sum(): lax.all_to_all(pieces, 'row', split_axis=0, concat_axis=0, tiled=True)]
  transfers between devices with their start and end apart: 8 -> 20, of which waited for: 8 -> 10; matrix products, arithmetic and copies ran while one was open for 17% -> 23% of each run, Pallas kernels for 0% -> 0%
where the time goes in v1:
time: 272 us; the launch traced here: 271 us
  waiting for transfers between devices  97.4 us (36%)
  starting transfers between devices  56.7 us (21%)
  matrix products  35.4 us (13%)
  blocking collectives  30.7 us (11%)
  local copies, waits for them, and re-layouts  28.9 us (11%)
  between operations  13.9 us (5%)
  other arithmetic  7.88 us (3%)
    all_gather x1, waiting for transfers between devices, token_panel(): return lax.all_gather(local_rows, 'row', axis=0, tiled=True)  49.7 us
    all_to_all x1, blocking collectives, token_panel_a2a(): lax.all_to_all(copies, 'row', split_axis=0, concat_axis=0, tiled=True)  30.7 us
    reduce_scatter x2, waiting for transfers between devices, width_split(): lax.psum_scatter(term.astype(jnp.bfloat16), 'col', scatter_dimension=0, t...  22.3 us
    all_to_all x1, starting transfers between devices, local(): lax.all_to_all(block_rows, 'col', split_axis=0, concat_axis=1, tiled=True)  18.8 us
    ppermute x8, starting transfers between devices, collect(): lax.ppermute(going_up, axis, [(d, (d + 1) % ways) for d in range(ways)])  14.7 us
    ppermute x8, waiting for transfers between devices, collect(): lax.ppermute(going_up, axis, [(d, (d + 1) % ways) for d in range(ways)])  13.2 us
    ppermute x6, starting transfers between devices, collect(): lax.ppermute(going_down, axis, [(d, (d - 1) % ways) for d in range(ways)])  11.9 us
    all_to_all x2, starting transfers between devices, unit_sum(): lax.all_to_all(pieces, 'row', split_axis=0, concat_axis=0, tiled=True)  11.1 us
  transfers between devices with their start and end apart: 20, of which 10 were waited for; matrix products, arithmetic and copies ran while one was open for 23% of the time, Pallas kernels for 0%

profile of v1, /device:TPU:1, one launch (start us, length us, event | category | flops | bytes accessed | tf_op | source)
XLA Modules:
  0.0 270.8 jit_solution(1200020371998142489)
XLA Ops:
  7.2 0.0 all-gather.2.cloned.1.call-start
  7.2 0.7 all-gather.2.cloned.1.call-update
  7.9 0.0 reduce-scatter.3.cloned.1.call-start
  8.0 49.7 %all-gather.2.cloned.1.call-done = bf16[2048,512]{1,0:T(8,128)(2,1)} async-done(((bf16[128,512]{1,0:T(8,128)(2,1)}), bf16[2048,512]{1,0:T(8,128)(2,1)}) %all-gather.2.cloned.1.call-update) | async-done | bytes 2097168 | tf_op jit(solution)/shard_map/all_gather | solution.py:30
  57.6 6.2 %convolution_convert_fusion.1 = bf16[2048,1024]{1,0:T(8,128)(2,1)} fusion(bf16[2048,512]{1,0:T(8,128)(2,1)} %all-gather.2.cloned.1.call-done, bf16[512,1024]{1,0:T(8,128)(2,1)} %param.5), kind=kOutput, calls=%fused_computation.3 | convolution fusion | flops 2149580800 | bytes 7340032 | tf_op jit(solution)/shard_map/dot_general | solution.py:54
  63.9 0.0 reduce-scatter.5.cloned.1.call-start
  63.9 0.8 copy-done.4
  64.8 0.2 broadcast_in_dim.2
  65.0 30.7 %all_to_all.38 = bf16[16,128,512]{2,1,0:T(8,128)(2,1)S(1)} all-to-all(bf16[16,128,512]{2,1,0:T(8,128)(2,1)S(1)} %broadcast_in_dim.2), channel_id=1, replica_groups=mesh['row'=16,'col'=8] {'row'}, dimensions={0} | all-to-all | bytes 4194304 | tf_op jit(solution)/shard_map/all_to_all | solution.py:37
  95.6 1.3 copy-done.1
  97.0 4.3 %convolution_convert_fusion = bf16[2048,1024]{1,0:T(8,128)(2,1)} fusion(bf16[2048,512]{1,0:T(8,128)(2,1)S(1)} %bitcast.21, bf16[1024,512]{1,0:T(8,128)(2,1)S(1)} %copy-done), kind=kOutput, calls=%fused_computation.2 | convolution fusion | flops 2149580800 | bytes 7340032 | tf_op jit(solution)/shard_map/dot_general | solution.py:45
  101.3 0.0 reduce-scatter.3.cloned.1.call-done
  101.4 2.6 broadcast.20.clone
  103.9 3.0 %constant_dynamic-update-slice_fusion.15 = (bf16[2048,1024]{1,0:T(8,128)(2,1)}, bf16[256,1024]{1,0:T(8,128)(2,1)S(1)}) fusion(bf16[2048,1024]{1,0:T(8,128)(2,1)} %broadcast.20.clone, s32[]{:T(128)S(6)} %select_n.77, bf16[256,1024]{1,0:T(8,128)(2,1)S(1)} %copy-done.2), kind=kLoop, calls=%fused_computation.70 | loop fusion | flops 17301504 | bytes 1572868 | tf_op jit(solution)/shard_map/dynamic_update_slice | solution.py:10
  106.9 4.2 %collective-permute-start = (bf16[256,1024]{1,0:T(8,128)(2,1)S(1)}, bf16[256,1024]{1,0:T(8,128)(2,1)}, u32[]{:S(2)}, u32[]{:S(2)}) collective-permute-start(bf16[256,1024]{1,0:T(8,128)(2,1)S(1)} %get-tuple-element.19), channel_id=1, source_target_pairs={{0,1},{1,2},{2,3},{3,4},{4,5},{5,6},{6,7},{7,0},{8,9},{9,10},{10,1... | collective-permute-start | bytes 1572872 | tf_op jit(solution)/shard_map/ppermute | solution.py:13
  111.1 10.8 %collective-permute-done = bf16[256,1024]{1,0:T(8,128)(2,1)} collective-permute-done((bf16[256,1024]{1,0:T(8,128)(2,1)S(1)}, bf16[256,1024]{1,0:T(8,128)(2,1)}, u32[]{:S(2)}, u32[]{:S(2)}) %collective-permute-start) | collective-permute-done | bytes 524320 | tf_op jit(solution)/shard_map/ppermute | solution.py:13
  121.9 2.6 collective-permute-start.2
  124.5 22.3 %reduce-scatter.5.cloned.1.call-done = bf16[256,1024]{1,0:T(8,128)(2,1)} async-done(((bf16[2048,1024]{1,0:T(8,128)(2,1)}), bf16[256,1024]{1,0:T(8,128)(2,1)}) %reduce-scatter.5.cloned.1.call-update) | async-done | bytes 524304 | tf_op jit(solution)/shard_map/reduce_scatter | solution.py:55
  146.8 2.5 broadcast.20.clone.1
  149.2 1.3 constant_dynamic-update-slice_fusion.7
  150.5 1.3 collective-permute-start.7
  151.8 1.0 collective-permute-start.8
  152.8 3.0 %collective-permute-start.3 = (bf16[256,1024]{1,0:T(8,128)(2,1)S(1)}, bf16[256,1024]{1,0:T(8,128)(2,1)S(1)}, u32[]{:S(2)}, u32[]{:S(2)}) collective-permute-start(bf16[256,1024]{1,0:T(8,128)(2,1)S(1)} %collective-permute-done.1), channel_id=1, source_target_pairs={{0,7},{1,0},{2,1},{3,2},{4,3},{5,4},{6,5},{7,6},{8,15},{9,8},{10,9... | collective-permute-start | bytes 1572872 | tf_op jit(solution)/shard_map/ppermute | solution.py:16
  155.7 2.2 collective-permute-done.7
  157.9 2.6 collective-permute-start.9
  160.5 0.3 collective-permute-done.8
  160.8 1.9 collective-permute-start.10
  162.7 3.6 %collective-permute-done.3 = bf16[256,1024]{1,0:T(8,128)(2,1)S(1)} collective-permute-done((bf16[256,1024]{1,0:T(8,128)(2,1)S(1)}, bf16[256,1024]{1,0:T(8,128)(2,1)S(1)}, u32[]{:S(2)}, u32[]{:S(2)}) %collective-permute-start.3) | collective-permute-done | bytes 524320 | tf_op jit(solution)/shard_map/ppermute | solution.py:16
  166.3 1.7 collective-permute-start.5
  168.0 1.9 constant_dynamic-update-slice_fusion.14
  169.9 0.0 collective-permute-start.6
  170.0 0.8 constant_dynamic-update-slice_fusion.13
  170.8 1.9 constant_dynamic-update-slice_fusion.12
  172.7 0.8 constant_dynamic-update-slice_fusion.11
  173.6 0.8 constant_dynamic-update-slice_fusion.10
  174.4 3.2 %collective-permute-done.5 = bf16[256,1024]{1,0:T(8,128)(2,1)S(1)} collective-permute-done((bf16[256,1024]{1,0:T(8,128)(2,1)S(1)}, bf16[256,1024]{1,0:T(8,128)(2,1)S(1)}, u32[]{:S(2)}, u32[]{:S(2)}) %collective-permute-start.5) | collective-permute-done | bytes 524320 | tf_op jit(solution)/shard_map/ppermute | solution.py:16
  177.6 0.8 constant_dynamic-update-slice_fusion.9
  178.4 0.8 constant_dynamic-update-slice_fusion.8
  179.2 5.8 %convolution_convert_fusion.3 = bf16[2048,512]{1,0:T(8,128)(2,1)} fusion(bf16[2048,1024]{1,0:T(8,128)(2,1)} %constant_dynamic-update-slice_fusion.8, bf16[1024,512]{1,0:T(8,128)(2,1)S(1)} %copy-done), kind=kOutput, calls=%fused_computation.5 | convolution fusion | flops 2148532224 | bytes 7340032 | tf_op jit(solution)/shard_map/dot_general | solution.py:65
  185.1 4.1 %all-to-all-start = ((bf16[16,128,512]{2,1,0:T(8,128)(2,1)}), bf16[16,128,512]{2,1,0:T(8,128)(2,1)S(1)}, u32[]{:S(2)}, u32[]{:S(2)}) async-start(bf16[16,128,512]{2,1,0:T(8,128)(2,1)} %bitcast.23), calls=%async_computation.1 | async-start | bytes 4194304 | tf_op jit(solution)/shard_map/all_to_all | solution.py:67
  189.2 1.7 collective-permute-start.11
  190.9 4.4 %collective-permute-start.12 = (bf16[256,1024]{1,0:T(8,128)(2,1)}, bf16[256,1024]{1,0:T(8,128)(2,1)S(1)}, u32[]{:S(2)}, u32[]{:S(2)}) collective-permute-start(bf16[256,1024]{1,0:T(8,128)(2,1)} %collective-permute-done.10), channel_id=1, source_target_pairs={{0,7},{1,0},{2,1},{3,2},{4,3},{5,4},{6,5},{7,6},{8,15},{9,8},{10,9... | collective-permute-start | bytes 1572872 | tf_op jit(solution)/shard_map/ppermute | solution.py:16
  195.4 1.9 constant_dynamic-update-slice_fusion.6
  197.2 0.1 collective-permute-done.11
  197.4 2.4 collective-permute-start.13
  199.7 1.9 constant_dynamic-update-slice_fusion.5
  201.6 1.9 constant_dynamic-update-slice_fusion.4
  203.5 1.9 constant_dynamic-update-slice_fusion.3
  205.4 0.8 constant_dynamic-update-slice_fusion.2
  206.2 0.8 constant_dynamic-update-slice_fusion.1
  207.0 0.8 constant_dynamic-update-slice_fusion
  207.9 5.9 %convolution_convert_fusion.2 = bf16[2048,512]{1,0:T(8,128)(2,1)} fusion(bf16[2048,1024]{1,0:T(8,128)(2,1)} %constant_dynamic-update-slice_fusion, bf16[512,1024]{1,0:T(8,128)(2,1)S(1)} %copy-done.6), kind=kOutput, calls=%fused_computation.4 | convolution fusion | flops 2148532224 | bytes 7340032 | tf_op jit(solution)/shard_map/dot_general | solution.py:45
  213.8 7.0 %all-to-all-start.3 = ((bf16[16,128,512]{2,1,0:T(8,128)(2,1)}), bf16[16,128,512]{2,1,0:T(8,128)(2,1)}, u32[]{:S(2)}, u32[]{:S(2)}) async-start(bf16[16,128,512]{2,1,0:T(8,128)(2,1)} %bitcast.24), calls=%async_computation.5 | async-start | bytes 4194304 | tf_op jit(solution)/shard_map/all_to_all | solution.py:67
  220.8 6.5 %convolution_bitcast_fusion = f32[512,1024]{0,1:T(8,128)} fusion(bf16[2048,1024]{1,0:T(8,128)(2,1)} %constant_dynamic-update-slice_fusion, bf16[2048,512]{1,0:T(8,128)(2,1)} %all-gather.2.cloned.1.call-done), kind=kOutput, calls=%fused_computation.12 | convolution fusion | flops 2147483648 | bytes 8388608 | tf_op jit(solution)/shard_map/dot_general | solution.py:84
  227.3 2.9 %copy.12 = f32[512,1024]{1,0:T(8,128)} copy(f32[512,1024]{0,1:T(8,128)} %convolution_bitcast_fusion) | data formatting | bytes 4194304
  230.2 6.6 %fusion.41 = f32[1024,512]{1,0:T(8,128)} fusion(bf16[2048,1024]{1,0:T(8,128)(2,1)} %constant_dynamic-update-slice_fusion.8, bf16[2048,512]{1,0:T(8,128)(2,1)} %bitcast.22), kind=kOutput, calls=%fused_computation.71 | convolution fusion | flops 2147483648 | bytes 8388608 | tf_op jit(solution)/shard_map/dot_general | solution.py:81
  236.8 0.3 convert_reduce_fusion.1
  237.1 0.7 add_convert_fusion.1
  237.8 1.7 all-to-all-done.3
  239.5 18.8 %all-to-all-start.1 = ((bf16[8,16,512]{2,1,0:T(8,128)(2,1)}), bf16[8,16,512]{2,1,0:T(8,128)(2,1)S(1)}, u32[]{:S(2)}, u32[]{:S(2)}) async-start(bf16[8,16,512]{2,1,0:T(8,128)(2,1)} %bitcast.1), calls=%async_computation.2 | async-start | bytes 262144 | tf_op jit(solution)/shard_map/all_to_all | solution.py:80
  258.3 1.9 convert_reduce_fusion
  260.2 0.7 add_convert_fusion
  260.9 2.7 all-to-all-done.1
  263.6 0.7 copy.13
  (25 shorter events, 0.1 us)
Async XLA Ops:
  7.2 89.8 %copy-start = (bf16[1024,512]{1,0:T(8,128)(2,1)S(1)}, bf16[1024,512]{1,0:T(8,128)(2,1)}, u32[]{:S(2)}) copy-start(bf16[1024,512]{1,0:T(8,128)(2,1)} %param.6) | copy-start | bytes 3145732
  7.2 50.5 %all-gather.2.cloned.1.call-start = ((), (), s32[]{:S(2)}) async-start(), calls=%async_computation.6 | async-start | bytes 2228224 | tf_op jit(solution)/shard_map/all_gather | solution.py:30
  7.9 93.4 %reduce-scatter.3.cloned.1.call-start = ((), (), s32[]{:S(2)}) async-start(), calls=%async_computation.7 | async-start | bytes 4718592 | tf_op jit(solution)/shard_map/reduce_scatter | solution.py:55
  63.9 0.9 copy-start.4
  63.9 82.9 %reduce-scatter.5.cloned.1.call-start = ((), (), s32[]{:S(2)}) async-start(), calls=%async_computation.8 | async-start | bytes 4718592 | tf_op jit(solution)/shard_map/reduce_scatter | solution.py:55
  95.6 1.3 copy-start.1
  101.4 2.6 copy-start.2
  106.9 15.0 %collective-permute-start = (bf16[256,1024]{1,0:T(8,128)(2,1)S(1)}, bf16[256,1024]{1,0:T(8,128)(2,1)}, u32[]{:S(2)}, u32[]{:S(2)}) collective-permute-start(bf16[256,1024]{1,0:T(8,128)(2,1)S(1)} %get-tuple-element.19), channel_id=1, source_target_pairs={{0,1},{1,2},{2,3},{3,4},{4,5},{5,6},{6,7},{7,0},{8,9},{9,10},{10,1... | collective-permute-start | bytes 1572872 | tf_op jit(solution)/shard_map/ppermute | solution.py:13
  111.1 41.7 %collective-permute-start.1 = (bf16[256,1024]{1,0:T(8,128)(2,1)S(1)}, bf16[256,1024]{1,0:T(8,128)(2,1)S(1)}, u32[]{:S(2)}, u32[]{:S(2)}) collective-permute-start(bf16[256,1024]{1,0:T(8,128)(2,1)S(1)} %get-tuple-element.19), channel_id=1, source_target_pairs={{0,7},{1,0},{2,1},{3,2},{4,3},{5,4},{6,5},{7,6},{8,15},{9,8},{10,9... | collective-permute-start | bytes 1572872 | tf_op jit(solution)/shard_map/ppermute | solution.py:16
  121.9 33.8 %collective-permute-start.2 = (bf16[256,1024]{1,0:T(8,128)(2,1)}, bf16[256,1024]{1,0:T(8,128)(2,1)}, u32[]{:S(2)}, u32[]{:S(2)}) collective-permute-start(bf16[256,1024]{1,0:T(8,128)(2,1)} %collective-permute-done), channel_id=1, source_target_pairs={{0,1},{1,2},{2,3},{3,4},{4,5},{5,6},{6,7},{7,0},{8,9},{9,10},{10,1... | collective-permute-start | bytes 1572872 | tf_op jit(solution)/shard_map/ppermute | solution.py:13
  146.8 2.5 copy-start.3
  150.5 7.4 %collective-permute-start.7 = (bf16[256,1024]{1,0:T(8,128)(2,1)S(1)}, bf16[256,1024]{1,0:T(8,128)(2,1)}, u32[]{:S(2)}, u32[]{:S(2)}) collective-permute-start(bf16[256,1024]{1,0:T(8,128)(2,1)S(1)} %get-tuple-element.17), channel_id=1, source_target_pairs={{0,1},{1,2},{2,3},{3,4},{4,5},{5,6},{6,7},{7,0},{8,9},{9,10},{10,1... | collective-permute-start | bytes 1572872 | tf_op jit(solution)/shard_map/ppermute | solution.py:13
  151.8 9.0 %collective-permute-start.8 = (bf16[256,1024]{1,0:T(8,128)(2,1)S(1)}, bf16[256,1024]{1,0:T(8,128)(2,1)}, u32[]{:S(2)}, u32[]{:S(2)}) collective-permute-start(bf16[256,1024]{1,0:T(8,128)(2,1)S(1)} %get-tuple-element.17), channel_id=1, source_target_pairs={{0,7},{1,0},{2,1},{3,2},{4,3},{5,4},{6,5},{7,6},{8,15},{9,8},{10,9... | collective-permute-start | bytes 1572872 | tf_op jit(solution)/shard_map/ppermute | solution.py:16
  152.8 13.6 %collective-permute-start.3 = (bf16[256,1024]{1,0:T(8,128)(2,1)S(1)}, bf16[256,1024]{1,0:T(8,128)(2,1)S(1)}, u32[]{:S(2)}, u32[]{:S(2)}) collective-permute-start(bf16[256,1024]{1,0:T(8,128)(2,1)S(1)} %collective-permute-done.1), channel_id=1, source_target_pairs={{0,7},{1,0},{2,1},{3,2},{4,3},{5,4},{6,5},{7,6},{8,15},{9,8},{10,9... | collective-permute-start | bytes 1572872 | tf_op jit(solution)/shard_map/ppermute | solution.py:16
  155.7 14.2 %collective-permute-start.4 = (bf16[256,1024]{1,0:T(8,128)(2,1)}, bf16[256,1024]{1,0:T(8,128)(2,1)S(1)}, u32[]{:S(2)}, u32[]{:S(2)}) collective-permute-start(bf16[256,1024]{1,0:T(8,128)(2,1)} %collective-permute-done.2), channel_id=1, source_target_pairs={{0,1},{1,2},{2,3},{3,4},{4,5},{5,6},{6,7},{7,0},{8,9},{9,10},{10,1... | collective-permute-start | bytes 1572872 | tf_op jit(solution)/shard_map/ppermute | solution.py:13
  157.9 31.3 %collective-permute-start.9 = (bf16[256,1024]{1,0:T(8,128)(2,1)}, bf16[256,1024]{1,0:T(8,128)(2,1)}, u32[]{:S(2)}, u32[]{:S(2)}) collective-permute-start(bf16[256,1024]{1,0:T(8,128)(2,1)} %collective-permute-done.7), channel_id=1, source_target_pairs={{0,1},{1,2},{2,3},{3,4},{4,5},{5,6},{6,7},{7,0},{8,9},{9,10},{10,1... | collective-permute-start | bytes 1572872 | tf_op jit(solution)/shard_map/ppermute | solution.py:13
  160.8 30.1 %collective-permute-start.10 = (bf16[256,1024]{1,0:T(8,128)(2,1)}, bf16[256,1024]{1,0:T(8,128)(2,1)}, u32[]{:S(2)}, u32[]{:S(2)}) collective-permute-start(bf16[256,1024]{1,0:T(8,128)(2,1)} %collective-permute-done.8), channel_id=1, source_target_pairs={{0,7},{1,0},{2,1},{3,2},{4,3},{5,4},{6,5},{7,6},{8,15},{9,8},{10,9... | collective-permute-start | bytes 1572872 | tf_op jit(solution)/shard_map/ppermute | solution.py:16
  166.3 11.2 %collective-permute-start.5 = (bf16[256,1024]{1,0:T(8,128)(2,1)S(1)}, bf16[256,1024]{1,0:T(8,128)(2,1)S(1)}, u32[]{:S(2)}, u32[]{:S(2)}) collective-permute-start(bf16[256,1024]{1,0:T(8,128)(2,1)S(1)} %collective-permute-done.3), channel_id=1, source_target_pairs={{0,7},{1,0},{2,1},{3,2},{4,3},{5,4},{6,5},{7,6},{8,15},{9,8},{10,9... | collective-permute-start | bytes 1572872 | tf_op jit(solution)/shard_map/ppermute | solution.py:16
  169.9 8.5 %collective-permute-start.6 = (bf16[256,1024]{1,0:T(8,128)(2,1)S(1)}, bf16[256,1024]{1,0:T(8,128)(2,1)S(1)}, u32[]{:S(2)}, u32[]{:S(2)}) collective-permute-start(bf16[256,1024]{1,0:T(8,128)(2,1)S(1)} %collective-permute-done.4), channel_id=1, source_target_pairs={{0,1},{1,2},{2,3},{3,4},{4,5},{5,6},{6,7},{7,0},{8,9},{9,10},{10,1... | collective-permute-start | bytes 1572872 | tf_op jit(solution)/shard_map/ppermute | solution.py:13
  185.1 28.7 %all-to-all-start = ((bf16[16,128,512]{2,1,0:T(8,128)(2,1)}), bf16[16,128,512]{2,1,0:T(8,128)(2,1)S(1)}, u32[]{:S(2)}, u32[]{:S(2)}) async-start(bf16[16,128,512]{2,1,0:T(8,128)(2,1)} %bitcast.23), calls=%async_computation.1 | async-start | bytes 4194304 | tf_op jit(solution)/shard_map/all_to_all | solution.py:67
  189.2 18.7 %copy-start.6 = (bf16[512,1024]{1,0:T(8,128)(2,1)S(1)}, bf16[512,1024]{1,0:T(8,128)(2,1)}, u32[]{:S(2)}) copy-start(bf16[512,1024]{1,0:T(8,128)(2,1)} %param.5) | copy-start | bytes 3145732
  189.2 8.1 %collective-permute-start.11 = (bf16[256,1024]{1,0:T(8,128)(2,1)}, bf16[256,1024]{1,0:T(8,128)(2,1)S(1)}, u32[]{:S(2)}, u32[]{:S(2)}) collective-permute-start(bf16[256,1024]{1,0:T(8,128)(2,1)} %collective-permute-done.9), channel_id=1, source_target_pairs={{0,1},{1,2},{2,3},{3,4},{4,5},{5,6},{6,7},{7,0},{8,9},{9,10},{10,1... | collective-permute-start | bytes 1572872 | tf_op jit(solution)/shard_map/ppermute | solution.py:13
  190.9 15.3 %collective-permute-start.12 = (bf16[256,1024]{1,0:T(8,128)(2,1)}, bf16[256,1024]{1,0:T(8,128)(2,1)S(1)}, u32[]{:S(2)}, u32[]{:S(2)}) collective-permute-start(bf16[256,1024]{1,0:T(8,128)(2,1)} %collective-permute-done.10), channel_id=1, source_target_pairs={{0,7},{1,0},{2,1},{3,2},{4,3},{5,4},{6,5},{7,6},{8,15},{9,8},{10,9... | collective-permute-start | bytes 1572872 | tf_op jit(solution)/shard_map/ppermute | solution.py:16
  197.4 9.7 %collective-permute-start.13 = (bf16[256,1024]{1,0:T(8,128)(2,1)S(1)}, bf16[256,1024]{1,0:T(8,128)(2,1)S(1)}, u32[]{:S(2)}, u32[]{:S(2)}) collective-permute-start(bf16[256,1024]{1,0:T(8,128)(2,1)S(1)} %collective-permute-done.11), channel_id=1, source_target_pairs={{0,1},{1,2},{2,3},{3,4},{4,5},{5,6},{6,7},{7,0},{8,9},{9,10},{10,1... | collective-permute-start | bytes 1572872 | tf_op jit(solution)/shard_map/ppermute | solution.py:13
  213.8 25.7 %all-to-all-start.3 = ((bf16[16,128,512]{2,1,0:T(8,128)(2,1)}), bf16[16,128,512]{2,1,0:T(8,128)(2,1)}, u32[]{:S(2)}, u32[]{:S(2)}) async-start(bf16[16,128,512]{2,1,0:T(8,128)(2,1)} %bitcast.24), calls=%async_computation.5 | async-start | bytes 4194304 | tf_op jit(solution)/shard_map/all_to_all | solution.py:67
  230.2 6.9 %copy-start.5 = (bf16[128,512]{1,0:T(8,128)(2,1)S(1)}, bf16[128,512]{1,0:T(8,128)(2,1)}, u32[]{:S(2)}) copy-start(bf16[128,512]{1,0:T(8,128)(2,1)} %param.4) | copy-start | bytes 393220
  239.5 24.1 %all-to-all-start.1 = ((bf16[8,16,512]{2,1,0:T(8,128)(2,1)}), bf16[8,16,512]{2,1,0:T(8,128)(2,1)S(1)}, u32[]{:S(2)}, u32[]{:S(2)}) async-start(bf16[8,16,512]{2,1,0:T(8,128)(2,1)} %bitcast.1), calls=%async_computation.2 | async-start | bytes 262144 | tf_op jit(solution)/shard_map/all_to_all | solution.py:80
Sparse Core Ops, SparseCore 0:
  10.2 47.4 all-gather.1
  64.0 35.4 reduce-scatter.2
  101.9 44.7 reduce-scatter.4
